TPU v7x, 32 devices: a whole 2x2x4 slice. The times are simulated.
32 devices in a mesh: dp: 4 (over y, x), loop: 8 (over z, core).
Axes of the slice: x: 2, y: 2, z: 4, core: 2. Of those that a mesh axis runs over, the one named last changes fastest.
Arguments:
- features: bfloat16 [24, 7, 7, 2048], P('loop'), may hold values from -6 to 6
- image_ids: int32 [24], P('loop'), may hold values from 0 to 15
- text_embeds: bfloat16 [16, 1152], P('loop'), may hold values from -6 to 6
- text_ids: int32 [16], replicated, may hold values from 0 to 15, each once
- depth_kernel: bfloat16 [7, 7, 2048], replicated, may hold values from -0.875 to 0.875
- depth_bias: float32 [2048], replicated, may hold values from -3 to 3
- norm_gain: float32 [2048], replicated, may hold values from 0.5 to 2
- w_up: bfloat16 [2048, 4096], P(None, 'dp'), may hold values from -0.125 to 0.125
- w_down: bfloat16 [2048, 4096], P(None, 'dp'), may hold values from -0.09375 to 0.09375
- projection: bfloat16 [2048, 1152], replicated, may hold values from -0.125 to 0.125
- logit_scale: float32 [1], replicated, may hold values from 4 to 16
- logit_bias: float32 [1], replicated, may hold values from -4 to -1
Outputs:
- row_loss: float32 [24], P('loop')
- grad_texts: float32 [16, 1152], P('loop')
- grad_kernel: float32 [7, 7, 2048], replicated
- grad_bias: float32 [2048], replicated
- grad_gain: float32 [2048], replicated
- grad_up: float32 [2048, 4096], P('loop', 'dp')
- grad_down: float32 [2048, 4096], P('loop', 'dp')
- grad_proj: float32 [2048, 1152], P(('dp', 'loop'))
Inputs may be any that keep to these rules, and one draw needn't show every extreme that they name: `image_ids`: each image's pair id names one text. `text_ids`: the 16 texts carry distinct pair ids.
All inputs are finite; a program needn't handle non-finite values.
Results may differ from a plain program's by a relative error of at most 0.0065.
Values sent between devices are 32-bit elements; how exact they have to be, the bound alone decides.
A program may use at most 192 MiB of HBM per device.

v0:
```python
import jax
import jax.numpy as jnp
import numpy as np
from jax import lax
from jax.sharding import PartitionSpec as P

GRID = 7
full_precision = lax.Precision.HIGHEST
half_root = 0.7071067811865476
density_factor = 0.3989422804014327


def shifted(shard, axis, by):
    count = lax.axis_size(axis)
    return lax.ppermute(shard, axis, [(i, (i + by) % count) for i in range(count)])


def gelu_value(values):
    return 0.5 * values * (1.0 + lax.erf(values * half_root))


def gelu_slope(values):
    cumulative = 0.5 * (1.0 + lax.erf(values * half_root))
    return cumulative + values * jnp.exp(-0.5 * values * values) * density_factor


def depthwise(images, kernel):
    side = kernel.shape[0]
    reach = (side - 1) // 2
    height = images.shape[1]
    width = images.shape[2]
    padded = jnp.pad(images, ((0, 0), (reach, reach), (reach, reach), (0, 0)))
    total = jnp.zeros(images.shape, jnp.float32)
    for row_off in range(side):
        for col_off in range(side):
            window = padded[:, row_off : row_off + height, col_off : col_off + width, :].astype(
                jnp.float32
            )
            total = total + window * kernel[row_off, col_off]
    return total


def kernel_grad(images, grad_conv, side):
    reach = (side - 1) // 2
    height = images.shape[1]
    width = images.shape[2]
    padded = jnp.pad(images, ((0, 0), (reach, reach), (reach, reach), (0, 0)))
    positions = np.arange(width)
    rows_out = []
    for row_off in range(side):
        slab = padded[:, row_off : row_off + height, :, :].astype(jnp.float32)
        cross = jnp.einsum("npsc,npqc->sqc", slab, grad_conv, precision=full_precision)
        cols_out = []
        for col_off in range(side):
            cols_out.append(jnp.sum(cross[positions + col_off, positions], axis=0))
        rows_out.append(jnp.stack(cols_out, axis=0))
    return jnp.stack(rows_out, axis=0)


def norm_parts(images, depth_kernel, depth_bias, norm_gain):
    conv_out = depthwise(images, depth_kernel.astype(jnp.float32)) + depth_bias
    centered = conv_out - jnp.mean(conv_out, axis=3, keepdims=True)
    inv_std = lax.rsqrt(jnp.mean(centered * centered, axis=3, keepdims=True) + 1e-06)
    unit_part = centered * inv_std
    normed = (unit_part * norm_gain).astype(jnp.bfloat16)
    return (unit_part, inv_std, normed)


def unit_rows(values):
    inverse = lax.rsqrt(jnp.sum(values * values, axis=1, keepdims=True) + 1e-06)
    return (values * inverse, inverse)


def conv_grads(images, depth_kernel, unit_part, inv_std, norm_gain, grad_normed):
    grad_gain = jnp.sum(grad_normed * unit_part, axis=(0, 1, 2))
    grad_unit = grad_normed * norm_gain
    grad_conv = inv_std * (
        grad_unit
        - jnp.mean(grad_unit, axis=3, keepdims=True)
        - unit_part * jnp.mean(grad_unit * unit_part, axis=3, keepdims=True)
    )
    grad_bias = jnp.sum(grad_conv, axis=(0, 1, 2))
    grad_kernel = kernel_grad(images, grad_conv, depth_kernel.shape[0])
    return (grad_kernel, grad_bias, grad_gain)


def on_device(
    features,
    image_ids,
    text_embeds,
    text_ids,
    depth_kernel,
    depth_bias,
    norm_gain,
    w_up,
    w_down,
    projection,
    logit_scale,
    logit_bias,
):
    image_rows = features.shape[0]
    channels = features.shape[3]
    hidden_share = w_up.shape[1]
    cell_count = GRID * GRID
    loop_count = lax.axis_size("loop")
    position = lax.axis_index("loop")
    unit_part, inv_std, normed = norm_parts(features, depth_kernel, depth_bias, norm_gain)
    normed_rows = normed.reshape(-1, channels)
    pre_act = jnp.dot(normed_rows, w_up, preferred_element_type=jnp.float32)
    hidden_mean = jnp.mean(
        gelu_value(pre_act).reshape(image_rows, cell_count, hidden_share), axis=1
    ).astype(jnp.bfloat16)
    mlp_part = lax.dot_general(
        hidden_mean, w_down, (((1,), (1,)), ((), ())), preferred_element_type=jnp.float32
    )
    mlp_pool = lax.psum(mlp_part, "dp")
    pooled = (jnp.mean(features.astype(jnp.float32), axis=(1, 2)) + mlp_pool).astype(jnp.bfloat16)
    embedding = jnp.dot(pooled, projection, preferred_element_type=jnp.float32)
    image_unit, image_inverse = unit_rows(embedding)
    text_unit, text_inverse = unit_rows(text_embeds.astype(jnp.float32))
    text_rows = text_embeds.shape[0]
    embed_width = text_embeds.shape[1]
    scale_value = logit_scale[0]
    bias_value = logit_bias[0]

    def pair_tile(block_unit, first_text):
        block_ids = lax.dynamic_slice_in_dim(text_ids, first_text, block_unit.shape[0])
        logits = (
            scale_value * jnp.dot(image_unit, block_unit.T, precision=full_precision) + bias_value
        )
        labels = jnp.where(image_ids[:, None] == block_ids[None, :], 1.0, -1.0).astype(jnp.float32)
        loss_part = -jnp.sum(jax.nn.log_sigmoid(labels * logits), axis=1)
        coeffs = -scale_value * labels * jax.nn.sigmoid(-labels * logits)
        return (loss_part, coeffs)

    def loop_turn(turn_index, carry_state):
        moving, loss_sum, grad_image = carry_state
        block_unit = moving[:text_rows]
        block_grad = moving[text_rows:]
        source = (position - turn_index) % loop_count
        loss_part, coeffs = pair_tile(block_unit, source * text_rows)
        grad_image = grad_image + jnp.dot(coeffs, block_unit, precision=full_precision)
        block_grad = block_grad + jnp.dot(coeffs.T, image_unit, precision=full_precision)
        stacked = jnp.concatenate([block_unit, block_grad], axis=0)
        moving = shifted(stacked, "loop", 1)
        return (moving, loss_sum + loss_part, grad_image)

    start_state = (
        jnp.concatenate([text_unit, jnp.zeros((text_rows, embed_width), jnp.float32)], axis=0),
        jnp.zeros((image_rows,), jnp.float32),
        jnp.zeros((image_rows, embed_width), jnp.float32),
    )
    moving, row_loss, grad_image = lax.fori_loop(0, loop_count, loop_turn, start_state)
    grad_text = moving[text_rows:]
    grad_texts = text_inverse * (
        grad_text - text_unit * jnp.sum(text_unit * grad_text, axis=1, keepdims=True)
    )
    grad_embed = (
        image_inverse
        * (grad_image - image_unit * jnp.sum(image_unit * grad_image, axis=1, keepdims=True))
    ).astype(jnp.bfloat16)
    grad_pooled = lax.dot_general(
        grad_embed, projection, (((1,), (1,)), ((), ())), preferred_element_type=jnp.float32
    ).astype(jnp.bfloat16)
    spread = jnp.dot(grad_pooled, w_down, preferred_element_type=jnp.float32) / cell_count
    grad_pre = (
        (gelu_slope(pre_act).reshape(image_rows, cell_count, hidden_share) * spread[:, None, :])
        .reshape(-1, hidden_share)
        .astype(jnp.bfloat16)
    )
    grad_normed = lax.dot_general(
        grad_pre, w_up, (((1,), (1,)), ((), ())), preferred_element_type=jnp.float32
    ).reshape(features.shape)
    kernel_part, bias_part, gain_part = conv_grads(
        features, depth_kernel, unit_part, inv_std, norm_gain, grad_normed
    )
    grad_kernel, grad_bias, grad_gain = lax.psum(
        (kernel_part, bias_part, gain_part), ("dp", "loop")
    )
    down_term = lax.dot_general(
        grad_pooled, hidden_mean, (((0,), (0,)), ((), ())), preferred_element_type=jnp.float32
    )
    row_share = channels // lax.axis_size("dp")
    pooled_share = lax.dynamic_slice_in_dim(pooled, lax.axis_index("dp") * row_share, row_share, 1)
    proj_term = lax.dot_general(
        pooled_share, grad_embed, (((0,), (0,)), ((), ())), preferred_element_type=jnp.float32
    )
    up_term = lax.dot_general(
        normed_rows, grad_pre, (((0,), (0,)), ((), ())), preferred_element_type=jnp.float32
    )
    grad_up, grad_down, grad_proj = (
        lax.psum_scatter(up_term, "loop", scatter_dimension=0, tiled=True),
        lax.psum_scatter(down_term, "loop", scatter_dimension=0, tiled=True),
        lax.psum_scatter(proj_term, "loop", scatter_dimension=0, tiled=True),
    )
    return (row_loss, grad_texts, grad_kernel, grad_bias, grad_gain, grad_up, grad_down, grad_proj)


def solution(mesh):
    placed = (
        P("loop", None, None, None),
        P("loop"),
        P("loop", None),
        P(),
        P(),
        P(),
        P(),
        P(None, "dp"),
        P(None, "dp"),
        P(),
        P(),
        P(),
    )
    return jax.shard_map(
        on_device,
        mesh=mesh,
        in_specs=placed,
        out_specs=(
            P("loop"),
            P("loop", None),
            P(),
            P(),
            P(),
            P("loop", "dp"),
            P("loop", "dp"),
            P(("dp", "loop"), None),
        ),
        check_vma=False,
    )
```

profile of v0, /device:TPU:1, one launch (start us, length us, event | category | flops | bytes accessed | tf_op | source)
XLA Modules:
  0.0 731.8 jit_solution(5146053782400025438)
XLA Ops:
  9.8 2.0 fusion.63
  11.8 2.1 fusion.62
  15.8 4.1 pad_slice_fusion
  20.8 12.0 %fusion.60 = (f32[3,7,7]{2,1,0:T(8,128)S(1)}, f32[3,7,7,2048]{3,2,1,0:T(8,128)S(1)}) fusion(f32[2048]{0:T(1024)} %param.167, f32[2048]{0:T(1024)} %bitcast.201, f32[2048]{0:T(1024)} %bitcast.200, f32[2048]{0:T(1024)} %bitcast.199, f32[2048]{0:T(1024)} %bitcast.198, f32[2048]{0:T(1024)} %bitcast.197, f32[2048]{0:T(1024)} %bitcast.196, ...), kind=kLoop, calls=%fused_computation.218 | loop fusion | flops 44556140 | bytes 2216524 | tf_op jit(solution)/shard_map/reduce_sum | solution.py:62
  35.7 4.3 multiply_multiply_fusion.1
  41.2 3.4 fusion.51
  44.6 13.7 %psum.28 = f32[3,2048]{1,0:T(4,128)S(1)} all-reduce(f32[3,2048]{1,0:T(4,128)S(1)} %fusion.51), channel_id=1, replica_groups=mesh['dp'=4,'loop'=8] {'dp'}, use_global_device_ids=true, to_apply=%region_5.6 | all-reduce | flops 6144 | bytes 49152 | tf_op jit(solution)/shard_map/psum | solution.py:116
  58.3 3.2 multiply_reduce_fusion.5
  61.6 55.7 %while.20 = (s32[]{:T(128)}, f32[4,1152]{1,0:T(4,128)S(1)}, f32[3]{0:T(128)S(1)}, f32[3,1152]{1,0:T(4,128)S(1)}, f32[]{:T(128)}, /*index=5*/s32[3]{0:T(128)S(1)}...) while((s32[]{:T(128)}, f32[4,1152]{1,0:T(4,128)S(1)}, ...), condition=%wide.region_9.10_spmd.clone, body=%wide.region_7.9_spmd.clone.sunk | while | flops 262864 | bytes 270863 | solution.py:153
  63.6 5.7 collective-permute-start
  72.0 2.4 collective-permute-start
  77.6 1.9 collective-permute-start
  79.9 2.7 collective-permute-done
  85.0 4.5 collective-permute-done
  91.9 4.6 collective-permute-done
  98.8 4.6 collective-permute-done
  105.8 4.6 collective-permute-done
  112.7 4.6 collective-permute-done
  117.6 3.8 convolution_convert_fusion
  125.3 4.9 multiply_reduce_fusion
  130.2 2.3 fusion.59
  132.5 14.9 %copy.168 = f32[3,7,7,2048]{1,2,0,3:T(8,128)} copy(f32[3,7,7,2048]{3,2,1,0:T(8,128)} %get-tuple-element.326) | data formatting | bytes 2408448 | tf_op jit(solution)/shard_map/mul | solution.py:77
  147.4 11.5 %copy.169 = bf16[3,7,13,2048]{2,1,0,3:T(8,128)(2,1)} copy(bf16[3,7,13,2048]{3,2,1,0:T(8,128)(2,1)S(1)} %copy-done.6) | data formatting | bytes 2236416 | tf_op jit(solution)/shard_map/slice | solution.py:51
  158.9 23.4 %convolution_bitcast_fusion.6 = f32[13,7,2048]{0,1,2:T(8,128)} fusion(f32[3,7,7,2048]{1,2,0,3:T(8,128)} %copy.168, bf16[3,7,13,2048]{2,1,0,3:T(8,128)(2,1)} %copy.169), kind=kOutput, calls=%fused_computation.133 | convolution fusion | flops 46964736 | bytes 3067904 | tf_op jit(solution)/shard_map/npsc,npqc->sqc/dot_general | solution.py:52
  182.3 5.3 copy.170
  190.2 13.0 %copy.178 = bf16[3,7,13,2048]{2,1,0,3:T(8,128)(2,1)} copy(bf16[3,7,13,2048]{3,2,1,0:T(8,128)(2,1)} %get-tuple-element.333) | data formatting | bytes 2236416 | tf_op jit(solution)/shard_map/slice | solution.py:51
  203.1 23.5 %convolution_bitcast_fusion.5 = f32[13,7,2048]{0,1,2:T(8,128)} fusion(f32[3,7,7,2048]{1,2,0,3:T(8,128)} %copy.168, bf16[3,7,13,2048]{2,1,0,3:T(8,128)(2,1)} %copy.178), kind=kOutput, calls=%fused_computation.132 | convolution fusion | flops 46964736 | bytes 3067904 | tf_op jit(solution)/shard_map/npsc,npqc->sqc/dot_general | solution.py:52
  226.6 5.3 copy.179
  246.2 13.0 %copy.187 = bf16[3,7,13,2048]{2,1,0,3:T(8,128)(2,1)} copy(bf16[3,7,13,2048]{3,2,1,0:T(8,128)(2,1)} %get-tuple-element.334) | data formatting | bytes 2236416 | tf_op jit(solution)/shard_map/slice | solution.py:51
  259.1 23.7 %convolution_bitcast_fusion.4 = f32[13,7,2048]{0,1,2:T(8,128)} fusion(f32[3,7,7,2048]{1,2,0,3:T(8,128)} %copy.168, bf16[3,7,13,2048]{2,1,0,3:T(8,128)(2,1)} %copy.187), kind=kOutput, calls=%fused_computation.131 | convolution fusion | flops 46964736 | bytes 3067904 | tf_op jit(solution)/shard_map/npsc,npqc->sqc/dot_general | solution.py:52
  282.8 5.3 copy.188
  296.8 13.0 %copy.196 = bf16[3,7,13,2048]{2,1,0,3:T(8,128)(2,1)} copy(bf16[3,7,13,2048]{3,2,1,0:T(8,128)(2,1)} %get-tuple-element.335) | data formatting | bytes 2236416 | tf_op jit(solution)/shard_map/slice | solution.py:51
  309.7 23.3 %convolution_bitcast_fusion.3 = f32[13,7,2048]{0,1,2:T(8,128)} fusion(f32[3,7,7,2048]{1,2,0,3:T(8,128)} %copy.168, bf16[3,7,13,2048]{2,1,0,3:T(8,128)(2,1)} %copy.196), kind=kOutput, calls=%fused_computation.130 | convolution fusion | flops 46964736 | bytes 3067904 | tf_op jit(solution)/shard_map/npsc,npqc->sqc/dot_general | solution.py:52
  333.1 5.3 copy.197
  347.0 11.5 %copy.205 = bf16[3,7,13,2048]{2,1,0,3:T(8,128)(2,1)} copy(bf16[3,7,13,2048]{3,2,1,0:T(8,128)(2,1)S(1)} %get-tuple-element.336) | data formatting | bytes 2236416 | tf_op jit(solution)/shard_map/slice | solution.py:51
  358.5 23.4 %convolution_bitcast_fusion.2 = f32[13,7,2048]{0,1,2:T(8,128)} fusion(f32[3,7,7,2048]{1,2,0,3:T(8,128)} %copy.168, bf16[3,7,13,2048]{2,1,0,3:T(8,128)(2,1)} %copy.205), kind=kOutput, calls=%fused_computation.129 | convolution fusion | flops 46964736 | bytes 3067904 | tf_op jit(solution)/shard_map/npsc,npqc->sqc/dot_general | solution.py:52
  381.9 5.3 copy.206
  392.3 11.5 %copy.214 = bf16[3,7,13,2048]{2,1,0,3:T(8,128)(2,1)} copy(bf16[3,7,13,2048]{3,2,1,0:T(8,128)(2,1)S(1)} %copy-done.5) | data formatting | bytes 2236416 | tf_op jit(solution)/shard_map/slice | solution.py:51
  403.8 23.4 %convolution_bitcast_fusion.1 = f32[13,7,2048]{0,1,2:T(8,128)} fusion(f32[3,7,7,2048]{1,2,0,3:T(8,128)} %copy.168, bf16[3,7,13,2048]{2,1,0,3:T(8,128)(2,1)} %copy.214), kind=kOutput, calls=%fused_computation.128 | convolution fusion | flops 46964736 | bytes 3067904 | tf_op jit(solution)/shard_map/npsc,npqc->sqc/dot_general | solution.py:52
  427.2 5.3 copy.215
  437.6 11.5 %copy.223 = bf16[3,7,13,2048]{2,1,0,3:T(8,128)(2,1)} copy(bf16[3,7,13,2048]{3,2,1,0:T(8,128)(2,1)S(1)} %copy-done.4) | data formatting | bytes 2236416 | tf_op jit(solution)/shard_map/slice | solution.py:51
  449.1 23.5 %convolution_bitcast_fusion = f32[13,7,2048]{0,1,2:T(8,128)} fusion(f32[3,7,7,2048]{1,2,0,3:T(8,128)} %copy.168, bf16[3,7,13,2048]{2,1,0,3:T(8,128)(2,1)} %copy.223), kind=kOutput, calls=%fused_computation.127 | convolution fusion | flops 46964736 | bytes 3067904 | tf_op jit(solution)/shard_map/npsc,npqc->sqc/dot_general | solution.py:52
  472.5 5.3 copy.224
  491.1 2.6 fusion.48
  494.9 4.5 fusion.65
  500.2 4.5 fusion.50
  505.4 41.1 %all-reduce.2 = (f32[2048]{0:T(1024)}, f32[2048]{0:T(1024)}) all-reduce(f32[2048]{0:T(1024)S(1)} %copy-done.67, f32[2048]{0:T(1024)S(1)} %copy-done.66), channel_id=1, replica_groups=mesh['dp'=4,'loop'=8] {'dp','loop'}, use_global_device_ids=true, to_apply=%region_65.66 | all-reduce | flops 4096 | bytes 32768 | tf_op jit(solution)/shard_map/psum | solution.py:177
  547.4 174.4 %all-reduce.5.cloned.1.call-done = f32[7,7,2048]{2,1,0:T(8,128)} async-done(((f32[7,7,2048]{2,1,0:T(8,128)}), f32[7,7,2048]{2,1,0:T(8,128)}) %all-reduce.5.cloned.1.call-update) | async-done | bytes 401424 | tf_op jit(solution)/shard_map/psum | solution.py:177
  (377 shorter events, 93.4 us)
Async XLA Ops:
  8.0 7.8 %copy-start.3 = (bf16[3,7,7,2048]{3,2,1,0:T(8,128)(2,1)S(1)}, bf16[3,7,7,2048]{3,2,1,0:T(8,128)(2,1)}, u32[]{:S(2)}) copy-start(bf16[3,7,7,2048]{3,2,1,0:T(8,128)(2,1)} %param.162) | copy-start | bytes 1806340
  8.0 713.9 %all-reduce.5.cloned.1.call-start = ((), (), s32[]{:S(2)}) async-start(), calls=%async_computation.3 | async-start | bytes 917504 | tf_op jit(solution)/shard_map/psum | solution.py:177
  15.8 4.1 copy-start.64
  20.1 13.1 %copy-start.71 = (f32[2]{0:T(128)}, f32[2]{0:T(128)S(1)}, u32[]{:S(2)}) copy-start(f32[2]{0:T(128)S(1)} %add_rsqrt_fusion.2) | copy-start | bytes 28
  20.8 12.4 %copy-start.57 = (f32[2048]{0:T(1024)S(1)}, f32[2048]{0:T(1024)}, u32[]{:S(2)}) copy-start(f32[2048]{0:T(1024)} %param.168) | copy-start | bytes 24580
  35.7 4.3 copy-start.1
  41.2 17.1 %copy-start.62 = (f32[3,2048]{1,0:T(4,128)S(1)}, f32[3,2048]{1,0:T(4,128)}, u32[]{:S(2)}) copy-start(f32[3,2048]{1,0:T(4,128)} %convert_reduce_fusion) | copy-start | bytes 73732
  61.5 59.8 %copy-start.16 = (f32[3,1152]{1,0:T(4,128)}, f32[3,1152]{1,0:T(4,128)S(1)}, u32[]{:S(2)}) copy-start(f32[3,1152]{1,0:T(4,128)S(1)} %get-tuple-element.390) | copy-start | bytes 41476
  61.6 59.8 %copy-start.68 = (f32[3]{0:T(128)}, f32[3]{0:T(128)S(1)}, u32[]{:S(2)}) copy-start(f32[3]{0:T(128)S(1)} %add_rsqrt_fusion.1) | copy-start | bytes 40
  63.6 6.6 collective-permute-start
  72.0 3.7 collective-permute-start
  77.6 5.0 collective-permute-start
  84.5 5.0 collective-permute-start
  91.5 5.0 collective-permute-start
  98.4 5.0 collective-permute-start
  105.4 5.0 collective-permute-start
  112.3 5.0 collective-permute-start
  117.3 4.1 copy-start.18
  117.3 4.1 copy-start.58
  117.3 4.1 copy-start.70
  117.5 4.5 copy-start
  125.2 5.1 copy-start.7
  132.5 14.9 %copy-start.6 = (bf16[3,7,13,2048]{3,2,1,0:T(8,128)(2,1)S(1)}, bf16[3,7,13,2048]{3,2,1,0:T(8,128)(2,1)}, u32[]{:S(2)}) copy-start(bf16[3,7,13,2048]{3,2,1,0:T(8,128)(2,1)} %get-tuple-element.332) | copy-start | bytes 3354628
  182.3 6.6 copy-start.14
  226.6 7.2 copy-start.13
  231.9 4.4 copy-start.12
  233.2 5.6 copy-start.11
  235.0 6.2 copy-start.10
  237.5 6.2 copy-start.9
  480.3 6.3 copy-start.49
  480.3 6.3 copy-start.48
  481.6 5.1 copy-start.50
  481.6 5.2 copy-start.51
  481.6 5.2 copy-start.52
  481.6 5.3 copy-start.53
  481.6 5.3 copy-start.54
  482.8 4.2 copy-start.24
  482.8 4.3 copy-start.20
  482.8 4.4 copy-start.21
  482.8 4.4 copy-start.22
  482.9 4.5 copy-start.23
  482.9 4.5 copy-start.25
  491.0 230.8 %reduce-scatter.8.cloned.1.call-start = ((), (), s32[]{:S(2)}) async-start(), calls=%async_computation.6 | async-start | bytes 2654208 | tf_op jit(solution)/shard_map/reduce_scatter | solution.py:194
  493.8 228.1 %reduce-scatter.4.cloned.1.call-start = ((), (), s32[]{:S(2)}) async-start(), calls=%async_computation.4 | async-start | bytes 9437184 | tf_op jit(solution)/shard_map/reduce_scatter | solution.py:192
  499.5 222.4 %reduce-scatter.6.cloned.1.call-start = ((), (), s32[]{:S(2)}) async-start(), calls=%async_computation.5 | async-start | bytes 9437184 | tf_op jit(solution)/shard_map/reduce_scatter | solution.py:193
  504.7 41.8 %copy-start.19 = (f32[4,1152]{1,0:T(4,128)S(1)}, f32[4,1152]{1,0:T(4,128)}, u32[]{:S(2)}) copy-start(f32[4,1152]{1,0:T(4,128)} %copy-done.18) | copy-start | bytes 55300
  504.7 41.9 %copy-start.65 = (bf16[2,1152]{1,0:T(2,128)(2,1)S(1)}, bf16[2,1152]{1,0:T(2,128)(2,1)}, u32[]{:S(2)}) copy-start(bf16[2,1152]{1,0:T(2,128)(2,1)} %param.164) | copy-start | bytes 13828
  504.7 41.8 %copy-start.72 = (f32[2]{0:T(128)S(1)}, f32[2]{0:T(128)}, u32[]{:S(2)}) copy-start(f32[2]{0:T(128)} %copy-done.71) | copy-start | bytes 28
  (41 other events, 101.3 us)
Sparse Core Ops, SparseCore 0:
  491.2 230.6 all-reduce.4
Sparse Core Ops, SparseCore 1:
  494.5 34.6 reduce-scatter.7
  532.0 89.7 reduce-scatter.3
  624.7 90.0 reduce-scatter.5
where the time goes:
time: 739 us; the launch traced here: 732 us
  matrix products  213 us (29%)
  local copies, waits for them, and re-layouts  210 us (28%)
  waiting for transfers between devices  202 us (27%)
  blocking collectives  54.8 us (7%)
  other arithmetic  22.8 us (3%)
  between operations  18.2 us (2%)
  starting transfers between devices  10.5 us (1%)
    psum x1, waiting for transfers between devices, on_device(): lax.psum((kernel_part, bias_part, gain_part), ('dp', 'loop'))  174 us
    dot_general x7, matrix products, kernel_grad(): jnp.einsum('npsc,npqc->sqc', slab, grad_conv, precision=full_precision)  164 us
    slice x8, local copies, waits for them, and re-layouts, kernel_grad(): slab = padded[:, row_off:row_off + height, :, :].astype(jnp.float32)  89 us
    gather x49, local copies, waits for them, and re-layouts, kernel_grad(): cols_out.append(jnp.sum(cross[positions + col_off, positions], axis=0))  52.7 us
    psum x1, blocking collectives, on_device(): lax.psum((kernel_part, bias_part, gain_part), ('dp', 'loop'))  41.1 us
    transpose x7, local copies, waits for them, and re-layouts, kernel_grad(): jnp.einsum('npsc,npqc->sqc', slab, grad_conv, precision=full_precision)  37.1 us
    ppermute x8, waiting for transfers between devices, shifted(): lax.ppermute(shard, axis, [(i, (i + by) % count) for i in range(count)])  27.2 us
    mul x1, local copies, waits for them, and re-layouts, conv_grads(): inv_std * (grad_unit - jnp.mean(grad_unit, axis=3, keepdims=True) - unit_...  14.9 us
  transfers between devices with their start and end apart: 12, of which 9 were waited for; matrix products, arithmetic and copies ran while one was open for 2% of the time, Pallas kernels for 0%

commit v1 on v0

--- a/solution.py
+++ b/solution.py
@@ -175,7 +175,7 @@
         features, depth_kernel, unit_part, inv_std, norm_gain, grad_normed
     )
     grad_kernel, grad_bias, grad_gain = lax.psum(
-        (kernel_part, bias_part, gain_part), ("dp", "loop")
+        lax.psum((kernel_part, bias_part, gain_part), "loop"), "dp"
     )
     down_term = lax.dot_general(
         grad_pooled, hidden_mean, (((0,), (0,)), ((), ())), preferred_element_type=jnp.float32

time: 739 us -> 832 us (1.13)
  waiting for transfers between devices: 202 us -> 297 us
    psum x1 -> x2, waiting for transfers between devices: 174 us -> 54.2 us  [the longest x1 54.2 us: on_device(): lax.psum((kernel_part, bias_part, gain_part), 'loop')]
    reduce_scatter x1, waiting for transfers between devices: 0.01 us -> 91.8 us  [on_device(): lax.psum_scatter(up_term, 'loop', scatter_dimension=0, tiled=True)]
    reduce_scatter x1, waiting for transfers between devices: 0.01 us -> 90.7 us  [on_device(): lax.psum_scatter(down_term, 'loop', scatter_dimension=0, tiled=True)]
    reduce_scatter x1, waiting for transfers between devices: 0.01 us -> 33.2 us  [on_device(): lax.psum_scatter(proj_term, 'loop', scatter_dimension=0, tiled=True)]
    psum x1 -> x2, blocking collectives: 41.1 us -> 37.1 us  [the longest x1 24.2 us: on_device(): lax.psum((kernel_part, bias_part, gain_part), 'loop')]
  transfers between devices with their start and end apart: 12 -> 13, of which waited for: 9 -> 12; matrix products, arithmetic and copies ran while one was open for 2% -> 2% of each run, Pallas kernels for 0% -> 0%
where the time goes in v1:
time: 832 us; the launch traced here: 822 us
  waiting for transfers between devices  297 us (36%)
  matrix products  213 us (26%)
  local copies, waits for them, and re-layouts  206 us (25%)
  blocking collectives  50.7 us (6%)
  other arithmetic  27.9 us (3%)
  between operations  16.2 us (2%)
  starting transfers between devices  10.5 us (1%)
    dot_general x7, matrix products, kernel_grad(): jnp.einsum('npsc,npqc->sqc', slab, grad_conv, precision=full_precision)  164 us
    reduce_scatter x1, waiting for transfers between devices, on_device(): lax.psum_scatter(up_term, 'loop', scatter_dimension=0, tiled=True)  91.8 us
    reduce_scatter x1, waiting for transfers between devices, on_device(): lax.psum_scatter(down_term, 'loop', scatter_dimension=0, tiled=True)  90.7 us
    slice x8, local copies, waits for them, and re-layouts, kernel_grad(): slab = padded[:, row_off:row_off + height, :, :].astype(jnp.float32)  89 us
    psum x1, waiting for transfers between devices, on_device(): lax.psum((kernel_part, bias_part, gain_part), 'loop')  54.2 us
    gather x49, local copies, waits for them, and re-layouts, kernel_grad(): cols_out.append(jnp.sum(cross[positions + col_off, positions], axis=0))  48.4 us
    transpose x7, local copies, waits for them, and re-layouts, kernel_grad(): jnp.einsum('npsc,npqc->sqc', slab, grad_conv, precision=full_precision)  37.1 us
    reduce_scatter x1, waiting for transfers between devices, on_device(): lax.psum_scatter(proj_term, 'loop', scatter_dimension=0, tiled=True)  33.2 us
  transfers between devices with their start and end apart: 13, of which 12 were waited for; matrix products, arithmetic and copies ran while one was open for 2% of the time, Pallas kernels for 0%

profile of v1, /device:TPU:1, one launch (start us, length us, event | category | flops | bytes accessed | tf_op | source)
XLA Modules:
  0.0 822.0 jit_solution(12358572630466767126)
XLA Ops:
  15.0 4.1 pad_slice_fusion
  20.0 12.0 %fusion.60 = (f32[3,7,7]{2,1,0:T(8,128)S(1)}, f32[3,7,7,2048]{3,2,1,0:T(8,128)S(1)}) fusion(f32[2048]{0:T(1024)} %param.167, f32[2048]{0:T(1024)} %bitcast.201, f32[2048]{0:T(1024)} %bitcast.200, f32[2048]{0:T(1024)} %bitcast.199, f32[2048]{0:T(1024)} %bitcast.198, f32[2048]{0:T(1024)} %bitcast.197, f32[2048]{0:T(1024)} %bitcast.196, ...), kind=kLoop, calls=%fused_computation.218 | loop fusion | flops 44556140 | bytes 2216524 | tf_op jit(solution)/shard_map/reduce_sum | solution.py:62
  34.9 4.3 multiply_multiply_fusion.1
  40.4 3.4 fusion.51
  43.8 13.7 %psum.49 = f32[3,2048]{1,0:T(4,128)S(1)} all-reduce(f32[3,2048]{1,0:T(4,128)S(1)} %fusion.51), channel_id=1, replica_groups=mesh['dp'=4,'loop'=8] {'dp'}, use_global_device_ids=true, to_apply=%region_5.6 | all-reduce | flops 6144 | bytes 49152 | tf_op jit(solution)/shard_map/psum | solution.py:116
  57.5 3.2 multiply_reduce_fusion.5
  60.8 55.7 %while.20 = (s32[]{:T(128)}, f32[4,1152]{1,0:T(4,128)S(1)}, f32[3]{0:T(128)S(1)}, f32[3,1152]{1,0:T(4,128)S(1)}, f32[]{:T(128)}, /*index=5*/s32[3]{0:T(128)S(1)}...) while((s32[]{:T(128)}, f32[4,1152]{1,0:T(4,128)S(1)}, ...), condition=%wide.region_9.10_spmd.clone, body=%wide.region_7.9_spmd.clone.sunk | while | flops 262864 | bytes 270863 | solution.py:153
  62.7 5.7 collective-permute-start
  71.2 2.4 collective-permute-start
  79.0 2.7 collective-permute-done
  84.2 4.5 collective-permute-done
  91.1 4.6 collective-permute-done
  98.0 4.6 collective-permute-done
  104.9 4.6 collective-permute-done
  111.9 4.6 collective-permute-done
  116.7 3.8 convolution_convert_fusion
  124.5 4.9 multiply_reduce_fusion
  131.7 14.9 %copy.168 = f32[3,7,7,2048]{1,2,0,3:T(8,128)} copy(f32[3,7,7,2048]{3,2,1,0:T(8,128)} %get-tuple-element.328) | data formatting | bytes 2408448 | tf_op jit(solution)/shard_map/mul | solution.py:77
  146.6 11.5 %copy.169 = bf16[3,7,13,2048]{2,1,0,3:T(8,128)(2,1)} copy(bf16[3,7,13,2048]{3,2,1,0:T(8,128)(2,1)S(1)} %copy-done.6) | data formatting | bytes 2236416 | tf_op jit(solution)/shard_map/slice | solution.py:51
  158.1 23.4 %convolution_bitcast_fusion.6 = f32[13,7,2048]{0,1,2:T(8,128)} fusion(f32[3,7,7,2048]{1,2,0,3:T(8,128)} %copy.168, bf16[3,7,13,2048]{2,1,0,3:T(8,128)(2,1)} %copy.169), kind=kOutput, calls=%fused_computation.133 | convolution fusion | flops 46964736 | bytes 3067904 | tf_op jit(solution)/shard_map/npsc,npqc->sqc/dot_general | solution.py:52
  181.5 5.3 copy.170
  189.3 13.0 %copy.178 = bf16[3,7,13,2048]{2,1,0,3:T(8,128)(2,1)} copy(bf16[3,7,13,2048]{3,2,1,0:T(8,128)(2,1)} %get-tuple-element.335) | data formatting | bytes 2236416 | tf_op jit(solution)/shard_map/slice | solution.py:51
  202.3 23.5 %convolution_bitcast_fusion.5 = f32[13,7,2048]{0,1,2:T(8,128)} fusion(f32[3,7,7,2048]{1,2,0,3:T(8,128)} %copy.168, bf16[3,7,13,2048]{2,1,0,3:T(8,128)(2,1)} %copy.178), kind=kOutput, calls=%fused_computation.132 | convolution fusion | flops 46964736 | bytes 3067904 | tf_op jit(solution)/shard_map/npsc,npqc->sqc/dot_general | solution.py:52
  225.7 5.3 copy.179
  245.3 13.0 %copy.187 = bf16[3,7,13,2048]{2,1,0,3:T(8,128)(2,1)} copy(bf16[3,7,13,2048]{3,2,1,0:T(8,128)(2,1)} %get-tuple-element.336) | data formatting | bytes 2236416 | tf_op jit(solution)/shard_map/slice | solution.py:51
  258.3 23.7 %convolution_bitcast_fusion.4 = f32[13,7,2048]{0,1,2:T(8,128)} fusion(f32[3,7,7,2048]{1,2,0,3:T(8,128)} %copy.168, bf16[3,7,13,2048]{2,1,0,3:T(8,128)(2,1)} %copy.187), kind=kOutput, calls=%fused_computation.131 | convolution fusion | flops 46964736 | bytes 3067904 | tf_op jit(solution)/shard_map/npsc,npqc->sqc/dot_general | solution.py:52
  282.0 5.3 copy.188
  295.9 13.0 %copy.196 = bf16[3,7,13,2048]{2,1,0,3:T(8,128)(2,1)} copy(bf16[3,7,13,2048]{3,2,1,0:T(8,128)(2,1)} %get-tuple-element.337) | data formatting | bytes 2236416 | tf_op jit(solution)/shard_map/slice | solution.py:51
  308.9 23.3 %convolution_bitcast_fusion.3 = f32[13,7,2048]{0,1,2:T(8,128)} fusion(f32[3,7,7,2048]{1,2,0,3:T(8,128)} %copy.168, bf16[3,7,13,2048]{2,1,0,3:T(8,128)(2,1)} %copy.196), kind=kOutput, calls=%fused_computation.130 | convolution fusion | flops 46964736 | bytes 3067904 | tf_op jit(solution)/shard_map/npsc,npqc->sqc/dot_general | solution.py:52
  332.2 5.3 copy.197
  346.2 11.5 %copy.205 = bf16[3,7,13,2048]{2,1,0,3:T(8,128)(2,1)} copy(bf16[3,7,13,2048]{3,2,1,0:T(8,128)(2,1)S(1)} %get-tuple-element.338) | data formatting | bytes 2236416 | tf_op jit(solution)/shard_map/slice | solution.py:51
  357.7 23.4 %convolution_bitcast_fusion.2 = f32[13,7,2048]{0,1,2:T(8,128)} fusion(f32[3,7,7,2048]{1,2,0,3:T(8,128)} %copy.168, bf16[3,7,13,2048]{2,1,0,3:T(8,128)(2,1)} %copy.205), kind=kOutput, calls=%fused_computation.129 | convolution fusion | flops 46964736 | bytes 3067904 | tf_op jit(solution)/shard_map/npsc,npqc->sqc/dot_general | solution.py:52
  381.1 5.3 copy.206
  390.8 11.5 %copy.214 = bf16[3,7,13,2048]{2,1,0,3:T(8,128)(2,1)} copy(bf16[3,7,13,2048]{3,2,1,0:T(8,128)(2,1)S(1)} %copy-done.5) | data formatting | bytes 2236416 | tf_op jit(solution)/shard_map/slice | solution.py:51
  402.4 23.4 %convolution_bitcast_fusion.1 = f32[13,7,2048]{0,1,2:T(8,128)} fusion(f32[3,7,7,2048]{1,2,0,3:T(8,128)} %copy.168, bf16[3,7,13,2048]{2,1,0,3:T(8,128)(2,1)} %copy.214), kind=kOutput, calls=%fused_computation.128 | convolution fusion | flops 46964736 | bytes 3067904 | tf_op jit(solution)/shard_map/npsc,npqc->sqc/dot_general | solution.py:52
  425.8 5.3 copy.215
  435.5 11.5 %copy.223 = bf16[3,7,13,2048]{2,1,0,3:T(8,128)(2,1)} copy(bf16[3,7,13,2048]{3,2,1,0:T(8,128)(2,1)S(1)} %copy-done.4) | data formatting | bytes 2236416 | tf_op jit(solution)/shard_map/slice | solution.py:51
  447.1 23.5 %convolution_bitcast_fusion = f32[13,7,2048]{0,1,2:T(8,128)} fusion(f32[3,7,7,2048]{1,2,0,3:T(8,128)} %copy.168, bf16[3,7,13,2048]{2,1,0,3:T(8,128)(2,1)} %copy.223), kind=kOutput, calls=%fused_computation.127 | convolution fusion | flops 46964736 | bytes 3067904 | tf_op jit(solution)/shard_map/npsc,npqc->sqc/dot_general | solution.py:52
  470.5 5.3 copy.224
  490.9 54.2 %all-reduce.7.cloned.1.call-done = f32[7,7,2048]{2,1,0:T(8,128)} async-done(((f32[7,7,2048]{2,1,0:T(8,128)}), f32[7,7,2048]{2,1,0:T(8,128)}) %all-reduce.7.cloned.1.call-update) | async-done | bytes 401424 | tf_op jit(solution)/shard_map/psum | solution.py:178
  545.2 2.6 fusion.48
  549.0 4.5 fusion.65
  554.3 4.5 fusion.50
  559.5 24.2 %all-reduce.2 = (f32[2048]{0:T(1024)S(1)}, f32[2048]{0:T(1024)S(1)}) all-reduce(f32[2048]{0:T(1024)S(1)} %copy-done.54, f32[2048]{0:T(1024)S(1)} %copy-done.53), channel_id=1, replica_groups=mesh['dp'=4,'loop'=8] {'loop'}, use_global_device_ids=true, to_apply=%region_66.67 | all-reduce | flops 4096 | bytes 32768 | tf_op jit(solution)/shard_map/psum | solution.py:178
  583.7 12.9 %all-reduce.3 = (f32[2048]{0:T(1024)}, f32[2048]{0:T(1024)}) all-reduce(f32[2048]{0:T(1024)S(1)} %get-tuple-element.323, f32[2048]{0:T(1024)S(1)} %get-tuple-element.324), channel_id=1, replica_groups=mesh['dp'=4,'loop'=8] {'dp'}, use_global_device_ids=true, to_apply=%region_67.68 | all-reduce | flops 4096 | bytes 32768 | tf_op jit(solution)/shard_map/psum | solution.py:177
  597.4 33.2 %reduce-scatter.8.cloned.1.call-done = f32[64,1152]{1,0:T(8,128)} async-done(((f32[512,1152]{1,0:T(8,128)}), f32[64,1152]{1,0:T(8,128)}) %reduce-scatter.8.cloned.1.call-update) | async-done | bytes 294928 | tf_op jit(solution)/shard_map/reduce_scatter | solution.py:194
  630.6 91.8 %reduce-scatter.4.cloned.1.call-done = f32[256,1024]{1,0:T(8,128)} async-done(((f32[2048,1024]{1,0:T(8,128)}), f32[256,1024]{1,0:T(8,128)}) %reduce-scatter.4.cloned.1.call-update) | async-done | bytes 1048592 | tf_op jit(solution)/shard_map/reduce_scatter | solution.py:192
  722.4 90.7 %reduce-scatter.6.cloned.1.call-done = f32[256,1024]{1,0:T(8,128)} async-done(((f32[2048,1024]{1,0:T(8,128)}), f32[256,1024]{1,0:T(8,128)}) %reduce-scatter.6.cloned.1.call-update) | async-done | bytes 1048592 | tf_op jit(solution)/shard_map/reduce_scatter | solution.py:193
  (355 shorter events, 102.5 us)
Async XLA Ops:
  7.2 7.8 copy-start.3
  7.2 537.9 %all-reduce.7.cloned.1.call-start = ((), (), s32[]{:S(2)}) async-start(), calls=%async_computation.3 | async-start | bytes 917504 | tf_op jit(solution)/shard_map/psum | solution.py:178
  19.3 13.1 %copy-start.58 = (f32[2]{0:T(128)}, f32[2]{0:T(128)S(1)}, u32[]{:S(2)}) copy-start(f32[2]{0:T(128)S(1)} %add_rsqrt_fusion.2) | copy-start | bytes 28
  20.0 12.4 %copy-start.44 = (f32[2048]{0:T(1024)S(1)}, f32[2048]{0:T(1024)}, u32[]{:S(2)}) copy-start(f32[2048]{0:T(1024)} %param.168) | copy-start | bytes 24580
  40.4 17.1 %copy-start.49 = (f32[3,2048]{1,0:T(4,128)S(1)}, f32[3,2048]{1,0:T(4,128)}, u32[]{:S(2)}) copy-start(f32[3,2048]{1,0:T(4,128)} %convert_reduce_fusion) | copy-start | bytes 73732
  60.7 59.8 %copy-start.16 = (f32[3,1152]{1,0:T(4,128)}, f32[3,1152]{1,0:T(4,128)S(1)}, u32[]{:S(2)}) copy-start(f32[3,1152]{1,0:T(4,128)S(1)} %get-tuple-element.392) | copy-start | bytes 41476
  60.7 59.8 %copy-start.55 = (f32[3]{0:T(128)}, f32[3]{0:T(128)S(1)}, u32[]{:S(2)}) copy-start(f32[3]{0:T(128)S(1)} %add_rsqrt_fusion.1) | copy-start | bytes 40
  62.7 6.6 collective-permute-start
  71.2 3.7 collective-permute-start
  76.8 5.0 collective-permute-start
  83.7 5.0 collective-permute-start
  90.6 5.0 collective-permute-start
  97.6 5.0 collective-permute-start
  104.5 5.0 collective-permute-start
  111.5 5.0 collective-permute-start
  131.7 14.9 %copy-start.6 = (bf16[3,7,13,2048]{3,2,1,0:T(8,128)(2,1)S(1)}, bf16[3,7,13,2048]{3,2,1,0:T(8,128)(2,1)}, u32[]{:S(2)}) copy-start(bf16[3,7,13,2048]{3,2,1,0:T(8,128)(2,1)} %get-tuple-element.334) | copy-start | bytes 3354628
  225.7 7.2 copy-start.13
  478.3 9.4 %copy-start.24 = (f32[7,2048]{1,0:T(8,128)S(1)}, f32[7,2048]{1,0:T(8,128)}, u32[]{:S(2)}) copy-start(f32[7,2048]{1,0:T(8,128)} %gather_fusion.7) | copy-start | bytes 172036
  478.4 9.5 %copy-start.20 = (f32[7,2048]{1,0:T(8,128)S(1)}, f32[7,2048]{1,0:T(8,128)}, u32[]{:S(2)}) copy-start(f32[7,2048]{1,0:T(8,128)} %gather_fusion.9) | copy-start | bytes 172036
  478.4 9.5 %copy-start.21 = (f32[7,2048]{1,0:T(8,128)S(1)}, f32[7,2048]{1,0:T(8,128)}, u32[]{:S(2)}) copy-start(f32[7,2048]{1,0:T(8,128)} %gather_fusion.10) | copy-start | bytes 172036
  478.4 9.6 %copy-start.22 = (f32[7,2048]{1,0:T(8,128)S(1)}, f32[7,2048]{1,0:T(8,128)}, u32[]{:S(2)}) copy-start(f32[7,2048]{1,0:T(8,128)} %gather_fusion.11) | copy-start | bytes 172036
  478.4 9.6 %copy-start.23 = (f32[7,2048]{1,0:T(8,128)S(1)}, f32[7,2048]{1,0:T(8,128)}, u32[]{:S(2)}) copy-start(f32[7,2048]{1,0:T(8,128)} %gather_fusion.12) | copy-start | bytes 172036
  478.4 9.6 %copy-start.25 = (f32[7,2048]{1,0:T(8,128)S(1)}, f32[7,2048]{1,0:T(8,128)}, u32[]{:S(2)}) copy-start(f32[7,2048]{1,0:T(8,128)} %gather_fusion.13) | copy-start | bytes 172036
  479.6 8.4 %copy-start.38 = (f32[7,2048]{1,0:T(8,128)S(1)}, f32[7,2048]{1,0:T(8,128)}, u32[]{:S(2)}) copy-start(f32[7,2048]{1,0:T(8,128)} %gather_fusion.14) | copy-start | bytes 172036
  479.6 8.5 %copy-start.36 = (f32[7,2048]{1,0:T(8,128)S(1)}, f32[7,2048]{1,0:T(8,128)}, u32[]{:S(2)}) copy-start(f32[7,2048]{1,0:T(8,128)} %gather_fusion.15) | copy-start | bytes 172036
  479.6 8.5 %copy-start.34 = (f32[7,2048]{1,0:T(8,128)S(1)}, f32[7,2048]{1,0:T(8,128)}, u32[]{:S(2)}) copy-start(f32[7,2048]{1,0:T(8,128)} %gather_fusion.16) | copy-start | bytes 172036
  479.7 8.6 %copy-start.32 = (f32[7,2048]{1,0:T(8,128)S(1)}, f32[7,2048]{1,0:T(8,128)}, u32[]{:S(2)}) copy-start(f32[7,2048]{1,0:T(8,128)} %gather_fusion.17) | copy-start | bytes 172036
  479.7 8.6 %copy-start.30 = (f32[7,2048]{1,0:T(8,128)S(1)}, f32[7,2048]{1,0:T(8,128)}, u32[]{:S(2)}) copy-start(f32[7,2048]{1,0:T(8,128)} %gather_fusion.18) | copy-start | bytes 172036
  479.7 8.6 %copy-start.28 = (f32[7,2048]{1,0:T(8,128)S(1)}, f32[7,2048]{1,0:T(8,128)}, u32[]{:S(2)}) copy-start(f32[7,2048]{1,0:T(8,128)} %gather_fusion.19) | copy-start | bytes 172036
  479.7 8.6 %copy-start.26 = (f32[7,2048]{1,0:T(8,128)S(1)}, f32[7,2048]{1,0:T(8,128)}, u32[]{:S(2)}) copy-start(f32[7,2048]{1,0:T(8,128)} %gather_fusion.20) | copy-start | bytes 172036
  479.7 8.7 %copy-start.39 = (f32[7,2048]{1,0:T(8,128)S(1)}, f32[7,2048]{1,0:T(8,128)}, u32[]{:S(2)}) copy-start(f32[7,2048]{1,0:T(8,128)} %gather_fusion.21) | copy-start | bytes 172036
  480.9 7.5 copy-start.37
  480.9 7.5 copy-start.35
  480.9 7.5 copy-start.33
  480.9 7.6 copy-start.31
  480.9 7.6 copy-start.29
  481.0 7.7 copy-start.27
  489.2 56.0 %copy-start.17 = (f32[3,1152]{1,0:T(4,128)S(1)}, f32[3,1152]{1,0:T(4,128)}, u32[]{:S(2)}) copy-start(f32[3,1152]{1,0:T(4,128)} %copy-done.16) | copy-start | bytes 41476
  489.2 56.0 %copy-start.46 = (f32[3,1152]{1,0:T(4,128)S(1)}, f32[3,1152]{1,0:T(4,128)}, u32[]{:S(2)}) copy-start(f32[3,1152]{1,0:T(4,128)} %copy-done.45) | copy-start | bytes 41476
  489.2 56.0 %copy-start.56 = (f32[3]{0:T(128)S(1)}, f32[3]{0:T(128)}, u32[]{:S(2)}) copy-start(f32[3]{0:T(128)} %copy-done.55) | copy-start | bytes 40
  489.2 56.0 %copy-start.61 = (f32[3]{0:T(128)S(1)}, f32[3]{0:T(128)}, u32[]{:S(2)}) copy-start(f32[3]{0:T(128)} %copy-done.60) | copy-start | bytes 40
  490.8 106.6 %all-reduce.9.cloned.1.call-start = ((), (), s32[]{:S(2)}) async-start(), calls=%async_computation.4 | async-start | bytes 917504 | tf_op jit(solution)/shard_map/psum | solution.py:177
  545.1 85.5 %reduce-scatter.8.cloned.1.call-start = ((), (), s32[]{:S(2)}) async-start(), calls=%async_computation.7 | async-start | bytes 2654208 | tf_op jit(solution)/shard_map/reduce_scatter | solution.py:194
  547.9 174.6 %reduce-scatter.4.cloned.1.call-start = ((), (), s32[]{:S(2)}) async-start(), calls=%async_computation.5 | async-start | bytes 9437184 | tf_op jit(solution)/shard_map/reduce_scatter | solution.py:192
  553.5 259.6 %reduce-scatter.6.cloned.1.call-start = ((), (), s32[]{:S(2)}) async-start(), calls=%async_computation.6 | async-start | bytes 9437184 | tf_op jit(solution)/shard_map/reduce_scatter | solution.py:193
  558.8 37.8 %copy-start.19 = (f32[4,1152]{1,0:T(4,128)S(1)}, f32[4,1152]{1,0:T(4,128)}, u32[]{:S(2)}) copy-start(f32[4,1152]{1,0:T(4,128)} %copy-done.18) | copy-start | bytes 55300
  558.8 37.8 %copy-start.52 = (bf16[2,1152]{1,0:T(2,128)(2,1)S(1)}, bf16[2,1152]{1,0:T(2,128)(2,1)}, u32[]{:S(2)}) copy-start(bf16[2,1152]{1,0:T(2,128)(2,1)} %param.164) | copy-start | bytes 13828
  558.8 37.8 %copy-start.59 = (f32[2]{0:T(128)S(1)}, f32[2]{0:T(128)}, u32[]{:S(2)}) copy-start(f32[2]{0:T(128)} %copy-done.58) | copy-start | bytes 28
  (29 other events, 91.7 us)
Sparse Core Ops, SparseCore 0:
  490.9 54.0 all-reduce.6
  548.4 45.2 all-reduce.8
  596.6 34.0 reduce-scatter.7
  633.4 89.0 reduce-scatter.3
  725.1 87.9 reduce-scatter.5
